TPU v7x, 256 devices: a whole 4x4x8 slice. The times are simulated.
256 devices in a mesh: span: 16 (over z, x_hi), sp: 8 (over y, x_lo), fsdp: 2 (over core).
Axes of the slice: x: 4 (x_hi: 2, x_lo: 2; x = x_hi * 2 + x_lo), y: 4, z: 8, core: 2. Of those that a mesh axis runs over, the one named last changes fastest.
Arguments:
- query_pre: bfloat16 [2, 16384, 3072], P('fsdp', ('span', 'sp')), may hold values from -12 to 12
- key_pre: bfloat16 [2, 16384, 3072], P('fsdp', ('span', 'sp')), may hold values from -12 to 12
- values: bfloat16 [2, 16384, 3072], P('fsdp', ('span', 'sp')), may hold values from -6 to 6
- cotangent: bfloat16 [2, 16384, 3072], P('fsdp', ('span', 'sp')), may hold values from -6 to 6
- gains: float32 [2, 3072], P(None, 'fsdp'), may hold values from 0.5 to 1.5
- frame_span: int32 [2, 16384], P('fsdp', 'span'), may hold values from 0 to 31, as said below
- denoise_steps: int32 [2, 32], P('fsdp'), may hold values from 1 to 4
Outputs:
- query_grad: bfloat16 [2, 16384, 3072], P('fsdp', ('span', 'sp'))
- key_grad: bfloat16 [2, 16384, 3072], P('fsdp', ('span', 'sp'))
- value_grad: bfloat16 [2, 16384, 3072], P('fsdp', ('span', 'sp'))
- gain_grad: float32 [2, 3072], P(None, 'fsdp')
Inputs may be any that keep to these rules, and one draw needn't show every extreme that they name: `frame_span`: never falls along a video. Group g (tokens g * 1024 to (g + 1) * 1024 - 1) holds frame spans 2 g and 2 g + 1, each from a quarter to three quarters of the group's tokens.
All inputs are finite; a program needn't handle non-finite values.
Results may differ from a plain program's by a relative error of at most 0.0081.
The roundings to bfloat16 on the way count: a program that leaves them out, or rounds other values in their place, can miss the bound.
Values may be sent and summed in bfloat16 or wider, within the bound.
No kernel may reach another device: no remote copies, remote signals or barrier semaphores. Data moves between devices by JAX's collectives and lax.ppermute only.
A program may use at most 128 MiB of HBM per device.

v0:
```python
import jax
import jax.numpy as jnp
from jax import lax
from jax.sharding import PartitionSpec as P

HDIM = 128
EPSILON = 1e-06
NEGATIVE = -1e30


def from_behind(value, axis, steps):
    count = lax.axis_size(axis)
    first, last = (max(0, -steps), min(count, count - steps))
    return lax.ppermute(value, axis, [(source, source + steps) for source in range(first, last)])


def normed(raw_rows, gain_row):
    wide = raw_rows.astype(jnp.float32)
    inverse_rms = lax.rsqrt(jnp.mean(wide * wide, axis=-1, keepdims=True) + EPSILON)
    normal_rows = wide * inverse_rms
    return (normal_rows, inverse_rms, (normal_rows * gain_row).astype(jnp.bfloat16))


def norm_backward(grad_rows, normal_rows, inverse_rms, gain_row):
    upstream = grad_rows.astype(jnp.float32)
    scaled = upstream * gain_row
    inner = jnp.mean(scaled * normal_rows, axis=-1, keepdims=True)
    result = (inverse_rms * (scaled - normal_rows * inner)).astype(jnp.bfloat16)
    return (result, jnp.sum(upstream * normal_rows, axis=0))


def across(left, right):
    return lax.dot_general(
        left, right, (((1,), (1,)), ((), ())), preferred_element_type=jnp.float32
    )


def downward(left, right):
    return lax.dot_general(
        left, right, (((0,), (0,)), ((), ())), preferred_element_type=jnp.float32
    )


def head_grads(
    query_head, grad_head, key_joined, value_joined, joined_mask, step_weight, own_width
):
    score_scale = HDIM ** (-0.5)
    scores = across(query_head, key_joined) * score_scale
    masked = jnp.where(joined_mask, scores, NEGATIVE)
    row_max = jnp.max(masked, axis=1)
    row_total = jnp.sum(jnp.exp(masked - row_max[:, None]), axis=1)
    log_total = row_max + jnp.log(row_total)
    grad_prob = across(grad_head, value_joined)
    probs = jnp.where(joined_mask, jnp.exp(scores - log_total[:, None]), 0.0)
    row_delta = jnp.sum(probs * grad_prob, axis=1)
    factor = step_weight[:, None]
    sgrad = (factor * probs * (grad_prob - row_delta[:, None])).astype(jnp.bfloat16)
    weights = (factor * probs).astype(jnp.bfloat16)
    query_part = jnp.dot(sgrad, key_joined, preferred_element_type=jnp.float32) * score_scale
    key_own_grad = downward(sgrad[:, :own_width], query_head) * score_scale
    value_own_grad = downward(weights[:, :own_width], grad_head)
    return (
        query_part,
        key_own_grad,
        value_own_grad,
        sgrad[:, own_width:],
        weights[:, own_width:],
        log_total,
        row_delta,
    )


def on_device(query_pre, key_pre, values, cotangent, gains, frame_span, denoise_steps):
    gain_full = lax.all_gather(gains, "fsdp", axis=1, tiled=True)
    q_normal, q_inverse, q_ready = normed(query_pre[0], gain_full[0])
    k_normal, k_inverse, k_ready = normed(key_pre[0], gain_full[1])
    heads_query, heads_key, heads_value, heads_grad = (
        lax.all_to_all(q_ready, "sp", split_axis=1, concat_axis=0, tiled=True),
        lax.all_to_all(k_ready, "sp", split_axis=1, concat_axis=0, tiled=True),
        lax.all_to_all(values[0], "sp", split_axis=1, concat_axis=0, tiled=True),
        lax.all_to_all(cotangent[0], "sp", split_axis=1, concat_axis=0, tiled=True),
    )
    head_count = heads_query.shape[1] // HDIM
    own_width = heads_query.shape[0]
    span_ids = frame_span[0]
    step_table = denoise_steps[0].astype(jnp.float32)
    matches = span_ids[:, None] == lax.iota(jnp.int32, step_table.shape[0])[None, :]
    step_weight = jnp.sum(jnp.where(matches, step_table[None, :], 0.0), axis=1)
    group_index = lax.axis_index("span")
    key_prev, value_prev = from_behind((heads_key, heads_value), "span", 1)
    own_mask = span_ids[None, :] <= span_ids[:, None]
    prev_open = group_index > 0
    prev_mask = jnp.broadcast_to(prev_open, own_mask.shape)
    joined_mask = jnp.concatenate([own_mask, prev_mask], axis=1)
    key_joined_all = jnp.concatenate([heads_key, key_prev], axis=0)
    value_joined_all = jnp.concatenate([heads_value, value_prev], axis=0)
    query_parts = []
    key_parts = []
    value_parts = []
    sgrad_list = []
    weight_list = []
    total_list = []
    delta_list = []
    for head_index in range(head_count):
        first = head_index * HDIM
        last = first + HDIM
        outcome = head_grads(
            heads_query[:, first:last],
            heads_grad[:, first:last],
            key_joined_all[:, first:last],
            value_joined_all[:, first:last],
            joined_mask,
            step_weight,
            own_width,
        )
        query_parts.append(outcome[0])
        key_parts.append(outcome[1])
        value_parts.append(outcome[2])
        sgrad_list.append(outcome[3])
        weight_list.append(outcome[4])
        total_list.append(outcome[5])
        delta_list.append(outcome[6])
    query_attn = jnp.concatenate(query_parts, axis=1)
    key_own = jnp.concatenate(key_parts, axis=1)
    value_own = jnp.concatenate(value_parts, axis=1)
    key_terms = []
    value_terms = []
    for head_index in range(head_count):
        first = head_index * HDIM
        last = first + HDIM
        key_terms.append(
            downward(sgrad_list[head_index], heads_query[:, first:last]) * HDIM ** (-0.5)
        )
        value_terms.append(downward(weight_list[head_index], heads_grad[:, first:last]))
    key_back, value_back = from_behind(
        (jnp.concatenate(key_terms, axis=1), jnp.concatenate(value_terms, axis=1)), "span", -1
    )
    key_attn = key_own + key_back
    value_attn = value_own + value_back
    query_tokens, key_tokens, value_tokens = (
        lax.all_to_all(
            query_attn.astype(jnp.bfloat16), "sp", split_axis=0, concat_axis=1, tiled=True
        ),
        lax.all_to_all(
            key_attn.astype(jnp.bfloat16), "sp", split_axis=0, concat_axis=1, tiled=True
        ),
        lax.all_to_all(
            value_attn.astype(jnp.bfloat16), "sp", split_axis=0, concat_axis=1, tiled=True
        ),
    )
    query_back, query_gain = norm_backward(query_tokens, q_normal, q_inverse, gain_full[0])
    key_back_rows, key_gain = norm_backward(key_tokens, k_normal, k_inverse, gain_full[1])
    partial_value = jnp.stack([query_gain, key_gain])
    summed = lax.psum(partial_value, ("span", "sp"))
    gain_grad = lax.psum_scatter(summed, "fsdp", scatter_dimension=1, tiled=True)
    return (query_back[None], key_back_rows[None], value_tokens[None], gain_grad)


def solution(mesh):
    placed = (
        P("fsdp", ("span", "sp"), None),
        P("fsdp", ("span", "sp"), None),
        P("fsdp", ("span", "sp"), None),
        P("fsdp", ("span", "sp"), None),
        P(None, "fsdp"),
        P("fsdp", "span"),
        P("fsdp", None),
    )
    return jax.shard_map(
        on_device,
        mesh=mesh,
        in_specs=placed,
        out_specs=(
            P("fsdp", ("span", "sp"), None),
            P("fsdp", ("span", "sp"), None),
            P("fsdp", ("span", "sp"), None),
            P(None, "fsdp"),
        ),
        check_vma=False,
    )
```

profile of v0, /device:TPU:0, one launch (start us, length us, event | category | flops | bytes accessed | tf_op | source)
XLA Modules:
  0.0 1031.0 jit_solution(12937883028764885410)
XLA Ops:
  7.2 2.4 copy.78
  9.5 4.2 all-to-all-start.2
  18.8 7.4 all-to-all-done.2
  26.2 3.5 all-to-all-start.1
  29.8 2.3 copy.80
  32.1 9.4 all-to-all-done.1
  41.5 4.3 all-to-all-start.3
  46.3 5.9 collective-permute-start
  53.5 6.6 all-to-all-done.3
  60.1 4.2 all-to-all-start
  65.1 2.3 copy.79
  67.4 2.3 copy.81
  69.7 2.9 collective-permute-start.1
  72.6 12.8 %all-to-all-done = bf16[128,8,384]{2,0,1:T(8,128)(2,1)} async-done(((bf16[128,8,384]{2,0,1:T(8,128)(2,1)}), bf16[128,8,384]{2,0,1:T(8,128)(2,1)}, u32[]{:S(2)}, u32[]{:S(2)}) %all-to-all-start) | async-done | bytes 786464 | tf_op jit(solution)/shard_map/all_to_all | solution.py:78
  85.4 2.3 fusion.75
  87.7 2.7 fusion.82
  90.4 9.0 fusion.9
  99.4 8.6 exponential_reduce_fusion.2
  108.0 5.4 fusion.68
  113.4 5.4 fusion.61
  118.9 20.2 %fusion.6 = (f32[1024]{0:T(1024)S(1)}, f32[1024]{0:T(1024)S(1)}, f32[1024]{0:T(1024)S(1)}, f32[2048,1024]{0,1:T(8,128)}) fusion(f32[1024]{0:T(1024)S(1)} %log_add_fusion.2, f32[1024,2048]{1,0:T(8,128)} %get-tuple-element.37, pred[1024,1024]{1,0:T(32,128)(4,1)S(1)} %broadcast_compare_fusion, pred[]{:T(512)S(6)} %gt.3, f32[2048,1024]{0,1:T(8,128)} %fusion.68, ...), kind=kOutput, calls=%fused_computation.18 | convolution fusion | flops 569373696 | bytes 53239808 | tf_op jit(solution)/shard_map/dot_general | solution.py:33
  139.1 12.5 %multiply_convert_fusion.2 = (bf16[1024,2048]{1,0:T(8,128)(2,1)S(1)}, bf16[1024,2048]{1,0:T(8,128)(2,1)S(1)}, bf16[1024,2048]{1,0:T(8,128)(2,1)S(1)}, bf16[1024,2048]{1,0:T(8,128)(2,1)S(1)}) fusion(f32[1024]{0:T(1024)S(1)} %select_reduce_fusion, f32[1024]{0:T(1024)S(1)} %log_add_fusion.2, f32[1024,2048]{1,0:T(8,128)} %get-tuple-element.37, ...), kind=kLoop, calls=%fused_computation.26 | loop fusion | flops 33554432 | bytes 51400704 | tf_op jit(solution)/shard_map/convert_element_type | solution.py:58
  157.2 2.6 fusion.47
  159.8 3.3 fusion.38
  163.1 2.5 fusion.53
  165.6 2.5 fusion.44
  168.2 4.9 multiply_convert_fusion.1
  173.1 3.2 fusion.50
  176.2 3.5 fusion.56
  179.7 2.3 fusion.58
  182.0 2.2 fusion.57
  185.2 4.3 all-to-all-start.4
  189.6 2.8 pad_maximum_fusion
  198.8 2.2 fusion.20
  201.0 2.5 fusion.41
  209.0 2.6 reshape.278
  211.6 21.7 %collective-permute-done.2 = f32[1024,384]{1,0:T(8,128)} collective-permute-done((f32[1024,384]{1,0:T(8,128)}, f32[1024,384]{1,0:T(8,128)}, u32[]{:S(2)}, u32[]{:S(2)}) %collective-permute-start.2) | collective-permute-done | bytes 1572896 | tf_op jit(solution)/shard_map/ppermute | solution.py:14
  233.3 2.6 fusion.36
  235.9 5.6 all-to-all-start.5
  241.5 2.7 multiply_convert_fusion.4
  244.2 19.0 %collective-permute-done.3 = f32[1024,384]{0,1:T(8,128)} collective-permute-done((f32[1024,384]{0,1:T(8,128)}, f32[1024,384]{0,1:T(8,128)}, u32[]{:S(2)}, u32[]{:S(2)}) %collective-permute-start.3) | collective-permute-done | bytes 1572896 | tf_op jit(solution)/shard_map/ppermute | solution.py:14
  263.2 2.9 copy_bitcast_fusion
  266.1 10.1 all-to-all-done.5
  276.2 4.2 all-to-all-start.6
  288.2 5.7 all-to-all-done.6
  293.9 2.3 copy.94
  296.2 37.5 %reduce-scatter.4.cloned.1.call-done = f32[1536,2]{1,0:T(8,128)} async-done(((f32[3072,2]{1,0:T(8,128)}), f32[1536,2]{1,0:T(8,128)}) %reduce-scatter.4.cloned.1.call-update) | async-done | bytes 12304
  335.0 688.9 %psum.8 = f32[2,1536]{1,0:T(2,128)} all-reduce(f32[2,1536]{1,0:T(2,128)S(1)} %copy.105), channel_id=1, replica_groups=mesh['span'=16,'sp'=8,'fsdp'=2] {'span','sp'}, use_global_device_ids=true, to_apply=%region_16.17 | all-reduce | flops 3072 | bytes 24576 | tf_op jit(solution)/shard_map/psum | solution.py:154
  (98 shorter events, 35.1 us)
Async XLA Ops:
  7.2 10.0 copy-start.7
  9.5 16.7 %all-to-all-start.2 = ((bf16[128,8,384]{0,2,1:T(8,128)(2,1)}), bf16[128,8,384]{0,2,1:T(8,128)(2,1)}, u32[]{:S(2)}, u32[]{:S(2)}) async-start(bf16[128,8,384]{0,2,1:T(8,128)(2,1)} %bitcast.7), calls=%async_computation.2 | async-start | bytes 1572864 | tf_op jit(solution)/shard_map/all_to_all | solution.py:80
  17.2 28.6 %copy-start.5 = (bf16[1,128,3072]{2,1,0:T(8,128)(2,1)S(1)}, bf16[1,128,3072]{2,1,0:T(8,128)(2,1)}, u32[]{:S(2)}) copy-start(bf16[1,128,3072]{2,1,0:T(8,128)(2,1)} %param.7) | copy-start | bytes 2359300
  26.2 15.2 %all-to-all-start.1 = ((bf16[128,8,384]{2,0,1:T(8,128)(2,1)}), bf16[128,8,384]{2,0,1:T(8,128)(2,1)S(1)}, u32[]{:S(2)}, u32[]{:S(2)}) async-start(bf16[128,8,384]{2,0,1:T(8,128)(2,1)} %multiply_convert_fusion.5), calls=%async_computation.1 | async-start | bytes 1572864 | tf_op jit(solution)/shard_map/all_to_all | solution.py:79
  41.5 22.9 %copy-start.20 = (s32[1,32]{1,0:T(1,128)S(1)}, s32[1,32]{1,0:T(1,128)}, u32[]{:S(2)}) copy-start(s32[1,32]{1,0:T(1,128)} %param.13) | copy-start | bytes 388
  41.5 22.9 %copy-start.19 = (s32[1,1024]{1,0:T(1,128)S(1)}, s32[1,1024]{1,0:T(1,128)}, u32[]{:S(2)}) copy-start(s32[1,1024]{1,0:T(1,128)} %param.12) | copy-start | bytes 12292
  41.5 18.7 %all-to-all-start.3 = ((bf16[128,8,384]{0,2,1:T(8,128)(2,1)}), bf16[128,8,384]{0,2,1:T(8,128)(2,1)}, u32[]{:S(2)}, u32[]{:S(2)}) async-start(bf16[128,8,384]{0,2,1:T(8,128)(2,1)} %bitcast.118), calls=%async_computation.3 | async-start | bytes 1572864 | tf_op jit(solution)/shard_map/all_to_all | solution.py:81
  46.0 6.1 copy-start.2
  46.3 39.1 %collective-permute-start = (bf16[1024,384]{1,0:T(8,128)(2,1)S(1)}, bf16[1024,384]{1,0:T(8,128)(2,1)}, u32[]{:S(2)}, u32[]{:S(2)}) collective-permute-start(bf16[1024,384]{1,0:T(8,128)(2,1)S(1)} %bitcast.91), channel_id=1, source_target_pairs={{0,16},{16,32},{32,48},{48,64},{64,80},{80,96},{96,112},{112,128},... | collective-permute-start | bytes 2359304 | tf_op jit(solution)/shard_map/ppermute | solution.py:14
  60.1 25.3 %all-to-all-start = ((bf16[128,8,384]{2,0,1:T(8,128)(2,1)}), bf16[128,8,384]{2,0,1:T(8,128)(2,1)}, u32[]{:S(2)}, u32[]{:S(2)}) async-start(bf16[128,8,384]{2,0,1:T(8,128)(2,1)} %multiply_convert_fusion.6), calls=%async_computation | async-start | bytes 1572864 | tf_op jit(solution)/shard_map/all_to_all | solution.py:78
  69.7 38.3 %collective-permute-start.1 = (bf16[1024,384]{1,0:T(8,128)(2,1)}, bf16[1024,384]{1,0:T(8,128)(2,1)}, u32[]{:S(2)}, u32[]{:S(2)}) collective-permute-start(bf16[1024,384]{1,0:T(8,128)(2,1)} %bitcast.102), channel_id=1, source_target_pairs={{0,16},{16,32},{32,48},{48,64},{64,80},{80,96},{96,112},{112,128},... | collective-permute-start | bytes 2359304 | tf_op jit(solution)/shard_map/ppermute | solution.py:14
  87.7 11.7 %copy-start.1 = (f32[1024,2048]{1,0:T(8,128)}, f32[1024,2048]{1,0:T(8,128)S(1)}, u32[]{:S(2)}) copy-start(f32[1024,2048]{1,0:T(8,128)S(1)} %fusion.75) | copy-start | bytes 25165828
  90.4 9.0 copy-start
  99.4 8.6 copy-start.4
  99.4 8.6 copy-start.13
  139.1 12.6 %copy-start.14 = (bf16[8,128,384]{2,1,0:T(8,128)(2,1)S(1)}, bf16[8,128,384]{2,1,0:T(8,128)(2,1)}, u32[]{:S(2)}) copy-start(bf16[8,128,384]{2,1,0:T(8,128)(2,1)} %copy.81) | copy-start | bytes 2359300
  151.6 5.6 copy-start.9
  153.3 14.8 %slice-start.2 = ((s8[8388608]{0:T(1024)(128)(4,1)}), s8[4194304]{0:T(1024)(128)(4,1)S(1)}, s32[]{:S(2)}) async-start(s8[8388608]{0:T(1024)(128)(4,1)} %bitcast.89), calls=%async_computation.11 | async-start | bytes 8388608
  155.9 12.2 %slice-start = ((s8[8388608]{0:T(1024)(128)(4,1)}), s8[4194304]{0:T(1024)(128)(4,1)S(1)}, s32[]{:S(2)}) async-start(s8[8388608]{0:T(1024)(128)(4,1)} %bitcast.87), calls=%async_computation.9 | async-start | bytes 8388608
  157.2 10.9 %slice-start.3 = ((s8[8388608]{0:T(1024)(128)(4,1)}), s8[4194304]{0:T(1024)(128)(4,1)S(1)}, s32[]{:S(2)}) async-start(s8[8388608]{0:T(1024)(128)(4,1)} %bitcast.89), calls=%async_computation.12 | async-start | bytes 8388608
  159.8 8.3 slice-start.1
  179.7 2.4 copy-start.10
  185.2 10.5 %copy-start.17 = (f32[1024,128]{0,1:T(8,128)S(1)}, f32[1024,128]{0,1:T(8,128)}, u32[]{:S(2)}) copy-start(f32[1024,128]{0,1:T(8,128)} %fusion.16) | copy-start | bytes 1572868
  185.2 10.5 %copy-start.18 = (f32[1024,128]{0,1:T(8,128)S(1)}, f32[1024,128]{0,1:T(8,128)}, u32[]{:S(2)}) copy-start(f32[1024,128]{0,1:T(8,128)} %fusion.12) | copy-start | bytes 1572868
  185.2 18.3 %all-to-all-start.4 = ((bf16[8,128,384]{2,1,0:T(8,128)(2,1)}), bf16[8,128,384]{2,1,0:T(8,128)(2,1)}, u32[]{:S(2)}, u32[]{:S(2)}) async-start(bf16[8,128,384]{2,1,0:T(8,128)(2,1)} %pad_maximum_fusion.2), calls=%async_computation.4 | async-start | bytes 1572864 | tf_op jit(solution)/shard_map/all_to_all | solution.py:141
  189.6 9.2 copy-start.12
  192.4 41.0 %collective-permute-start.2 = (f32[1024,384]{1,0:T(8,128)}, f32[1024,384]{1,0:T(8,128)}, u32[]{:S(2)}, u32[]{:S(2)}) collective-permute-start(f32[1024,384]{1,0:T(8,128)} %pad_maximum_fusion), channel_id=1, source_target_pairs={{16,0},{32,16},{48,32},{64,48},{80,64},{96,80},{112,96},{128,112},... | collective-permute-start | bytes 4718600 | tf_op jit(solution)/shard_map/ppermute | solution.py:14
  195.8 5.3 copy-start.11
  197.0 6.5 copy-start.3
  197.0 66.2 %collective-permute-start.3 = (f32[1024,384]{0,1:T(8,128)}, f32[1024,384]{0,1:T(8,128)}, u32[]{:S(2)}, u32[]{:S(2)}) collective-permute-start(f32[1024,384]{0,1:T(8,128)} %pad_maximum_fusion.1), channel_id=1, source_target_pairs={{16,0},{32,16},{48,32},{64,48},{80,64},{96,80},{112,96},{128,112},... | collective-permute-start | bytes 4718600 | tf_op jit(solution)/shard_map/ppermute | solution.py:14
  205.6 27.8 %copy-start.15 = (f32[1024,128]{1,0:T(8,128)S(1)}, f32[1024,128]{1,0:T(8,128)}, u32[]{:S(2)}) copy-start(f32[1024,128]{1,0:T(8,128)} %fusion.38) | copy-start | bytes 1572868
  205.6 27.7 %copy-start.16 = (f32[1024,128]{1,0:T(8,128)S(1)}, f32[1024,128]{1,0:T(8,128)}, u32[]{:S(2)}) copy-start(f32[1024,128]{1,0:T(8,128)} %fusion.44) | copy-start | bytes 1572868
  209.0 32.5 %copy-start.6 = (bf16[1,128,3072]{2,1,0:T(8,128)(2,1)S(1)}, bf16[1,128,3072]{2,1,0:T(8,128)(2,1)}, u32[]{:S(2)}) copy-start(bf16[1,128,3072]{2,1,0:T(8,128)(2,1)} %param.7) | copy-start | bytes 2359300
  235.9 40.3 %all-to-all-start.5 = ((bf16[8,128,384]{2,1,0:T(8,128)(2,1)}), bf16[8,128,384]{2,1,0:T(8,128)(2,1)S(1)}, u32[]{:S(2)}, u32[]{:S(2)}) async-start(bf16[8,128,384]{2,1,0:T(8,128)(2,1)} %bitcast.119), calls=%async_computation.5 | async-start | bytes 1572864 | tf_op jit(solution)/shard_map/all_to_all | solution.py:144
  276.2 17.6 %all-to-all-start.6 = ((bf16[8,128,384]{1,2,0:T(8,128)(2,1)}), bf16[8,128,384]{1,2,0:T(8,128)(2,1)}, u32[]{:S(2)}, u32[]{:S(2)}) async-start(bf16[8,128,384]{1,2,0:T(8,128)(2,1)} %copy_bitcast_fusion), calls=%async_computation.6 | async-start | bytes 1572864 | tf_op jit(solution)/shard_map/all_to_all | solution.py:147
  280.5 53.2 %reduce-scatter.4.cloned.1.call-start = ((), (), s32[]{:S(2)}) async-start(), calls=%async_computation.8 | async-start | bytes 2359296
  281.5 5.3 copy-start.8
Sparse Core Ops, SparseCore 0:
  287.0 46.5 reduce-scatter.3
where the time goes:
time: 1040 us; the launch traced here: 1030 us
  blocking collectives  691 us (66%)
  waiting for transfers between devices  130 us (12%)
  matrix products  79.4 us (8%)
  other arithmetic  48.8 us (5%)
  starting transfers between devices  42.3 us (4%)
  local copies, waits for them, and re-layouts  24.5 us (2%)
  between operations  14.8 us (1%)
    psum x1, blocking collectives, on_device(): summed = lax.psum(partial_value, ('span', 'sp'))  689 us
    dot_general x6, matrix products, across(): lax.dot_general(left, right, (((1,), (1,)), ((), ())), preferred_element_...  45 us
    ppermute x4, waiting for transfers between devices, from_behind(): lax.ppermute(value, axis, [(source, source + steps) for source in range(f...  40.7 us
    unnamed x2, waiting for transfers between devices  37.5 us
    dot_general x12, matrix products, downward(): lax.dot_general(left, right, (((0,), (0,)), ((), ())), preferred_element_...  26.4 us
  transfers between devices with their start and end apart: 12, of which 9 were waited for; matrix products, arithmetic and copies ran while one was open for 7% of the time, Pallas kernels for 0%

commit v1 on v0

--- a/solution.py
+++ b/solution.py
@@ -6,6 +6,12 @@
 HDIM = 128
 EPSILON = 1e-06
 NEGATIVE = -1e30
+
+
+def gather_and_add(x, axis):
+    shards = lax.all_gather(x, axis, axis=0, tiled=False)
+    acc = shards.sum(axis=0)
+    return acc
 
 
 def from_behind(value, axis, steps):
@@ -151,7 +157,7 @@
     query_back, query_gain = norm_backward(query_tokens, q_normal, q_inverse, gain_full[0])
     key_back_rows, key_gain = norm_backward(key_tokens, k_normal, k_inverse, gain_full[1])
     partial_value = jnp.stack([query_gain, key_gain])
-    summed = lax.psum(partial_value, ("span", "sp"))
+    summed = gather_and_add(partial_value, ("span", "sp"))
     gain_grad = lax.psum_scatter(summed, "fsdp", scatter_dimension=1, tiled=True)
     return (query_back[None], key_back_rows[None], value_tokens[None], gain_grad)
 

time: 1040 us -> 962 us (0.925)
  blocking collectives: 691 us -> 2.02 us
  waiting for transfers between devices: 130 us -> 744 us
  matrix products: 79.4 us -> 67.6 us
    psum x1 -> x0, blocking collectives: 689 us -> none  [on_device(): summed = lax.psum(partial_value, ('span', 'sp'))]
    all_gather x0 -> x1, waiting for transfers between devices: none -> 628 us  [gather_and_add(): shards = lax.all_gather(x, axis, axis=0, tiled=False)]
    unnamed x2 -> x3, waiting for transfers between devices: 37.5 us -> 7.35 us
  transfers between devices with their start and end apart: 12 -> 13, of which waited for: 9 -> 10; matrix products, arithmetic and copies ran while one was open for 7% -> 8% of each run, Pallas kernels for 0% -> 0%
where the time goes in v1:
time: 962 us; the launch traced here: 953 us
  waiting for transfers between devices  744 us (77%)
  matrix products  67.6 us (7%)
  other arithmetic  55.7 us (6%)
  starting transfers between devices  39.7 us (4%)
  local copies, waits for them, and re-layouts  28.9 us (3%)
  between operations  14.9 us (2%)
    all_gather x1, waiting for transfers between devices, gather_and_add(): shards = lax.all_gather(x, axis, axis=0, tiled=False)  628 us
    ppermute x4, waiting for transfers between devices, from_behind(): lax.ppermute(value, axis, [(source, source + steps) for source in range(f...  50.4 us
    dot_general x6, matrix products, across(): lax.dot_general(left, right, (((1,), (1,)), ((), ())), preferred_element_...  43.5 us
    convert_element_type x2, other arithmetic, head_grads(): weights = (factor * probs).astype(jnp.bfloat16)  22.1 us
    dot_general x12, matrix products, downward(): lax.dot_general(left, right, (((0,), (0,)), ((), ())), preferred_element_...  20.4 us
  transfers between devices with their start and end apart: 13, of which 10 were waited for; matrix products, arithmetic and copies ran while one was open for 8% of the time, Pallas kernels for 0%

profile of v1, /device:TPU:0, one launch (start us, length us, event | category | flops | bytes accessed | tf_op | source)
XLA Modules:
  0.0 952.7 jit_solution(16917617218460601127)
XLA Ops:
  7.2 2.4 copy.78
  9.5 3.8 all-to-all-start.2
  13.4 2.0 all_gather.9
  19.3 7.0 all-to-all-done.2
  26.3 3.5 all-to-all-start.1
  31.0 10.9 %all-to-all-done.1 = bf16[128,8,384]{2,0,1:T(8,128)(2,1)S(1)} async-done(((bf16[128,8,384]{2,0,1:T(8,128)(2,1)}), bf16[128,8,384]{2,0,1:T(8,128)(2,1)S(1)}, u32[]{:S(2)}, u32[]{:S(2)}) %all-to-all-start.1) | async-done | bytes 786464 | tf_op jit(solution)/shard_map/all_to_all | solution.py:85
  41.8 4.3 all-to-all-start.3
  46.7 4.7 collective-permute-start
  52.7 7.8 all-to-all-done.3
  60.5 4.2 all-to-all-start
  65.5 1.9 copy.79
  67.4 2.3 copy.81
  69.7 2.5 collective-permute-start.1
  72.2 13.6 %all-to-all-done = bf16[128,8,384]{2,0,1:T(8,128)(2,1)} async-done(((bf16[128,8,384]{2,0,1:T(8,128)(2,1)}), bf16[128,8,384]{2,0,1:T(8,128)(2,1)}, u32[]{:S(2)}, u32[]{:S(2)}) %all-to-all-start) | async-done | bytes 786464 | tf_op jit(solution)/shard_map/all_to_all | solution.py:84
  85.8 2.4 fusion.75
  88.2 2.4 fusion.82
  90.6 9.8 %fusion.9 = (f32[1024]{0:T(1024)S(1)}, f32[1024]{0:T(1024)S(1)}, f32[1024]{0:T(1024)S(1)}, f32[1024,2048]{1,0:T(8,128)}) fusion(pred[1024,1024]{1,0:T(32,128)(4,1)S(1)} %broadcast_compare_fusion, pred[]{:T(512)S(6)} %gt.3, f32[1024,2048]{1,0:T(8,128)S(1)} %fusion.82, f32[1024,2048]{1,0:T(8,128)S(1)} %fusion.75, bf16[1024,384]{1,0:T(8,128)(2,1)S(1)} %bitcast.96, ...), kind=kOutput, calls=%fused_computation.27 | convolution fusion | flops 556790784 | bytes 28061696 | tf_op jit(solution)/shard_map/dot_general | solution.py:39
  100.4 8.5 exponential_reduce_fusion.2
  109.0 5.4 fusion.68
  114.4 5.4 fusion.61
  119.8 18.1 %fusion.6 = (f32[1024]{0:T(1024)S(1)}, f32[1024]{0:T(1024)S(1)}, f32[1024]{0:T(1024)S(1)}, f32[2048,1024]{0,1:T(8,128)}) fusion(f32[1024]{0:T(1024)S(1)} %log_add_fusion.2, f32[1024,2048]{1,0:T(8,128)} %get-tuple-element.37, pred[1024,1024]{1,0:T(32,128)(4,1)S(1)} %broadcast_compare_fusion, pred[]{:T(512)S(6)} %gt.3, f32[2048,1024]{0,1:T(8,128)} %fusion.68, ...), kind=kOutput, calls=%fused_computation.18 | convolution fusion | flops 569373696 | bytes 53239808 | tf_op jit(solution)/shard_map/dot_general | solution.py:39
  137.9 10.1 %multiply_convert_fusion.1 = (bf16[1024,2048]{1,0:T(8,128)(2,1)}, bf16[1024,2048]{1,0:T(8,128)(2,1)}) fusion(f32[1024]{0:T(1024)S(1)} %select_reduce_fusion, f32[1024]{0:T(1024)S(1)} %get-tuple-element.40, f32[1024,2048]{1,0:T(8,128)} %copy-done.1, pred[1024,1024]{1,0:T(32,128)(4,1)} %copy-done.3, pred[]{:T(512)S(6)} %gt.3, f32[1024]{0:T(1024)S(1)} %get-tuple-element.18, ...), kind=kLoop, calls=%fused_computation.25 | loop fusion | flops 16777216 | bytes 26226688 | tf_op jit(solution)/shard_map/convert_element_type | solution.py:64
  151.9 2.4 copy-done.2
  154.3 12.0 %multiply_convert_fusion.2 = (bf16[1024,2048]{1,0:T(8,128)(2,1)}, bf16[1024,2048]{1,0:T(8,128)(2,1)}, bf16[1024,2048]{1,0:T(8,128)(2,1)}, bf16[1024,2048]{1,0:T(8,128)(2,1)}) fusion(f32[1024]{0:T(1024)S(1)} %select_reduce_fusion, f32[1024]{0:T(1024)S(1)} %log_add_fusion.2, f32[1024,2048]{1,0:T(8,128)S(1)} %bitcast.92, pred[1024,1024]{1,0:T(32,128)(4,1)} %copy-done.3, ...), kind=kLoop, calls=%fused_computation.26 | loop fusion | flops 33554432 | bytes 51400704 | tf_op jit(solution)/shard_map/convert_element_type | solution.py:64
  166.3 2.5 fusion.47
  168.8 2.3 fusion.53
  171.2 1.8 fusion.50
  180.5 4.2 all-to-all-start.4
  184.7 2.5 fusion.38
  187.2 2.3 fusion.44
  191.4 21.0 %collective-permute-done.2 = f32[1024,384]{1,0:T(8,128)} collective-permute-done((f32[1024,384]{1,0:T(8,128)}, f32[1024,384]{1,0:T(8,128)}, u32[]{:S(2)}, u32[]{:S(2)}) %collective-permute-start.2) | collective-permute-done | bytes 1572896 | tf_op jit(solution)/shard_map/ppermute | solution.py:20
  212.4 2.5 fusion.36
  214.9 8.2 all-to-all-done.4
  223.0 4.2 all-to-all-start.5
  227.5 2.0 multiply_reduce_fusion.1
  229.6 11.1 %all-to-all-done.5 = bf16[8,128,384]{2,1,0:T(8,128)(2,1)} async-done(((bf16[8,128,384]{2,1,0:T(8,128)(2,1)}), bf16[8,128,384]{2,1,0:T(8,128)(2,1)}, u32[]{:S(2)}, u32[]{:S(2)}) %all-to-all-start.5) | async-done | bytes 786464 | tf_op jit(solution)/shard_map/all_to_all | solution.py:150
  240.7 2.0 multiply_reduce_fusion
  243.4 2.2 fusion.16
  245.6 2.1 fusion.12
  255.0 2.1 copy.85
  259.9 29.3 %collective-permute-done.3 = f32[1024,384]{0,1:T(8,128)} collective-permute-done((f32[1024,384]{0,1:T(8,128)}, f32[1024,384]{0,1:T(8,128)}, u32[]{:S(2)}, u32[]{:S(2)}) %collective-permute-start.3) | collective-permute-done | bytes 1572896 | tf_op jit(solution)/shard_map/ppermute | solution.py:20
  289.3 2.6 copy_bitcast_fusion
  291.8 4.9 all-to-all-start.6
  298.0 2.1 copy.92
  301.7 627.7 %all-gather.4.cloned.1.call-done = f32[128,2,3072]{2,1,0:T(2,128)} async-done(((f32[1,2,3072]{2,1,0:T(2,128)}), f32[128,2,3072]{2,1,0:T(2,128)}) %all-gather.4.cloned.1.call-update) | async-done | bytes 3145744 | tf_op jit(solution)/shard_map/all_gather | solution.py:12
  929.4 2.8 reduce_sum.139
  936.3 7.3 reduce-scatter.4.cloned.1.call-done
  943.7 2.0 copy.105
  (117 shorter events, 38.8 us)
Async XLA Ops:
  7.2 9.6 %copy-start.15 = (bf16[1,128,3072]{2,1,0:T(8,128)(2,1)S(1)}, bf16[1,128,3072]{2,1,0:T(8,128)(2,1)}, u32[]{:S(2)}) copy-start(bf16[1,128,3072]{2,1,0:T(8,128)(2,1)} %param.8) | copy-start | bytes 2359300
  9.5 20.3 %copy-start.26 = (bf16[1,128,3072]{2,1,0:T(8,128)(2,1)S(1)}, bf16[1,128,3072]{2,1,0:T(8,128)(2,1)}, u32[]{:S(2)}) copy-start(bf16[1,128,3072]{2,1,0:T(8,128)(2,1)} %param.10) | copy-start | bytes 2359300
  9.5 16.7 %all-to-all-start.2 = ((bf16[128,8,384]{0,2,1:T(8,128)(2,1)}), bf16[128,8,384]{0,2,1:T(8,128)(2,1)S(1)}, u32[]{:S(2)}, u32[]{:S(2)}) async-start(bf16[128,8,384]{0,2,1:T(8,128)(2,1)} %bitcast.7), calls=%async_computation.2 | async-start | bytes 1572864 | tf_op jit(solution)/shard_map/all_to_all | solution.py:86
  16.8 1.1 copy-start.7
  16.8 29.4 %copy-start.13 = (bf16[1,128,3072]{2,1,0:T(8,128)(2,1)S(1)}, bf16[1,128,3072]{2,1,0:T(8,128)(2,1)}, u32[]{:S(2)}) copy-start(bf16[1,128,3072]{2,1,0:T(8,128)(2,1)} %param.7) | copy-start | bytes 2359300
  26.2 26.5 %copy-start.25 = (bf16[128,8,384]{0,2,1:T(8,128)(2,1)}, bf16[128,8,384]{0,2,1:T(8,128)(2,1)S(1)}, u32[]{:S(2)}) copy-start(bf16[128,8,384]{0,2,1:T(8,128)(2,1)S(1)} %all-to-all-done.2) | copy-start | bytes 2359300
  26.3 15.6 %all-to-all-start.1 = ((bf16[128,8,384]{2,0,1:T(8,128)(2,1)}), bf16[128,8,384]{2,0,1:T(8,128)(2,1)S(1)}, u32[]{:S(2)}, u32[]{:S(2)}) async-start(bf16[128,8,384]{2,0,1:T(8,128)(2,1)} %multiply_convert_fusion.5), calls=%async_computation.1 | async-start | bytes 1572864 | tf_op jit(solution)/shard_map/all_to_all | solution.py:85
  41.8 48.7 %copy-start.4 = (bf16[128,8,384]{2,0,1:T(8,128)(2,1)}, bf16[128,8,384]{2,0,1:T(8,128)(2,1)S(1)}, u32[]{:S(2)}) copy-start(bf16[128,8,384]{2,0,1:T(8,128)(2,1)S(1)} %all-to-all-done.1) | copy-start | bytes 2359300
  41.8 22.9 %copy-start.28 = (s32[1,32]{1,0:T(1,128)S(1)}, s32[1,32]{1,0:T(1,128)}, u32[]{:S(2)}) copy-start(s32[1,32]{1,0:T(1,128)} %param.13) | copy-start | bytes 388
  41.8 22.9 %copy-start.27 = (s32[1,1024]{1,0:T(1,128)S(1)}, s32[1,1024]{1,0:T(1,128)}, u32[]{:S(2)}) copy-start(s32[1,1024]{1,0:T(1,128)} %param.12) | copy-start | bytes 12292
  41.8 18.7 %all-to-all-start.3 = ((bf16[128,8,384]{0,2,1:T(8,128)(2,1)}), bf16[128,8,384]{0,2,1:T(8,128)(2,1)}, u32[]{:S(2)}, u32[]{:S(2)}) async-start(bf16[128,8,384]{0,2,1:T(8,128)(2,1)} %bitcast.10), calls=%async_computation.3 | async-start | bytes 1572864 | tf_op jit(solution)/shard_map/all_to_all | solution.py:87
  46.4 5.0 copy-start.9
  46.7 39.1 %collective-permute-start = (bf16[1024,384]{1,0:T(8,128)(2,1)S(1)}, bf16[1024,384]{1,0:T(8,128)(2,1)S(1)}, u32[]{:S(2)}, u32[]{:S(2)}) collective-permute-start(bf16[1024,384]{1,0:T(8,128)(2,1)S(1)} %bitcast.93), channel_id=1, source_target_pairs={{0,16},{16,32},{32,48},{48,64},{64,80},{80,96},{96,112},{112,128},... | collective-permute-start | bytes 2359304 | tf_op jit(solution)/shard_map/ppermute | solution.py:20
  60.5 25.3 %all-to-all-start = ((bf16[128,8,384]{2,0,1:T(8,128)(2,1)}), bf16[128,8,384]{2,0,1:T(8,128)(2,1)}, u32[]{:S(2)}, u32[]{:S(2)}) async-start(bf16[128,8,384]{2,0,1:T(8,128)(2,1)} %multiply_convert_fusion.6), calls=%async_computation | async-start | bytes 1572864 | tf_op jit(solution)/shard_map/all_to_all | solution.py:84
  65.5 54.3 %copy-start.3 = (pred[1024,1024]{1,0:T(32,128)(4,1)}, pred[1024,1024]{1,0:T(32,128)(4,1)S(1)}, u32[]{:S(2)}) copy-start(pred[1024,1024]{1,0:T(32,128)(4,1)S(1)} %broadcast_compare_fusion) | copy-start | bytes 3145732
  69.7 39.3 %collective-permute-start.1 = (bf16[1024,384]{1,0:T(8,128)(2,1)S(1)}, bf16[1024,384]{1,0:T(8,128)(2,1)}, u32[]{:S(2)}, u32[]{:S(2)}) collective-permute-start(bf16[1024,384]{1,0:T(8,128)(2,1)S(1)} %bitcast.104), channel_id=1, source_target_pairs={{0,16},{16,32},{32,48},{48,64},{64,80},{80,96},{96,112},{112,128},... | collective-permute-start | bytes 2359304 | tf_op jit(solution)/shard_map/ppermute | solution.py:20
  85.8 4.8 copy-start.11
  88.2 12.2 %copy-start = (f32[1024,2048]{1,0:T(8,128)}, f32[1024,2048]{1,0:T(8,128)S(1)}, u32[]{:S(2)}) copy-start(f32[1024,2048]{1,0:T(8,128)S(1)} %fusion.75) | copy-start | bytes 25165828
  90.6 9.8 %copy-start.1 = (f32[1024,2048]{1,0:T(8,128)}, f32[1024,2048]{1,0:T(8,128)S(1)}, u32[]{:S(2)}) copy-start(f32[1024,2048]{1,0:T(8,128)S(1)} %fusion.82) | copy-start | bytes 25165828
  100.4 8.6 copy-start.23
  137.9 10.1 %slice-start = ((s8[8388608]{0:T(1024)(128)(4,1)}), s8[4194304]{0:T(1024)(128)(4,1)S(1)}, s32[]{:S(2)}) async-start(s8[8388608]{0:T(1024)(128)(4,1)} %bitcast.89), calls=%async_computation.10 | async-start | bytes 8388608
  137.9 11.6 %slice-start.2 = ((s8[8388608]{0:T(1024)(128)(4,1)}), s8[4194304]{0:T(1024)(128)(4,1)S(1)}, s32[]{:S(2)}) async-start(s8[8388608]{0:T(1024)(128)(4,1)} %bitcast.91), calls=%async_computation.12 | async-start | bytes 8388608
  137.9 12.8 %slice-start.1 = ((s8[8388608]{0:T(1024)(128)(4,1)}), s8[4194304]{0:T(1024)(128)(4,1)S(1)}, s32[]{:S(2)}) async-start(s8[8388608]{0:T(1024)(128)(4,1)} %bitcast.89), calls=%async_computation.11 | async-start | bytes 8388608
  137.9 14.0 %slice-start.3 = ((s8[8388608]{0:T(1024)(128)(4,1)}), s8[4194304]{0:T(1024)(128)(4,1)S(1)}, s32[]{:S(2)}) async-start(s8[8388608]{0:T(1024)(128)(4,1)} %bitcast.91), calls=%async_computation.13 | async-start | bytes 8388608
  137.9 16.4 %copy-start.2 = (f32[2048,1024]{0,1:T(8,128)S(1)}, f32[2048,1024]{0,1:T(8,128)}, u32[]{:S(2)}) copy-start(f32[2048,1024]{0,1:T(8,128)} %fusion.68) | copy-start | bytes 25165828
  166.3 4.9 copy-start.21
  171.1 4.6 copy-start.5
  171.2 4.6 copy-start.12
  171.2 4.6 copy-start.19
  173.0 4.0 copy-start.6
  174.3 38.1 %collective-permute-start.2 = (f32[1024,384]{1,0:T(8,128)}, f32[1024,384]{1,0:T(8,128)}, u32[]{:S(2)}, u32[]{:S(2)}) collective-permute-start(f32[1024,384]{1,0:T(8,128)} %pad_maximum_fusion), channel_id=1, source_target_pairs={{16,0},{32,16},{48,32},{64,48},{80,64},{96,80},{112,96},{128,112},... | collective-permute-start | bytes 4718600 | tf_op jit(solution)/shard_map/ppermute | solution.py:20
  180.5 42.5 %all-to-all-start.4 = ((bf16[8,128,384]{2,1,0:T(8,128)(2,1)}), bf16[8,128,384]{2,1,0:T(8,128)(2,1)}, u32[]{:S(2)}, u32[]{:S(2)}) async-start(bf16[8,128,384]{2,1,0:T(8,128)(2,1)} %pad_maximum_fusion.2), calls=%async_computation.4 | async-start | bytes 1572864 | tf_op jit(solution)/shard_map/all_to_all | solution.py:147
  184.7 4.8 copy-start.22
  189.6 38.0 %copy-start.10 = (f32[16,8,8,384]{3,2,1,0:T(8,128)S(1)}, f32[16,8,8,384]{3,2,1,0:T(8,128)}, u32[]{:S(2)}) copy-start(f32[16,8,8,384]{3,2,1,0:T(8,128)} %copy-done.9) | copy-start | bytes 4718596
  191.4 49.3 %copy-start.8 = (f32[16,8,8,384]{3,2,1,0:T(8,128)S(1)}, f32[16,8,8,384]{3,2,1,0:T(8,128)}, u32[]{:S(2)}) copy-start(f32[16,8,8,384]{3,2,1,0:T(8,128)} %copy-done.7) | copy-start | bytes 4718596
  223.0 17.6 %all-to-all-start.5 = ((bf16[8,128,384]{2,1,0:T(8,128)(2,1)}), bf16[8,128,384]{2,1,0:T(8,128)(2,1)}, u32[]{:S(2)}, u32[]{:S(2)}) async-start(bf16[8,128,384]{2,1,0:T(8,128)(2,1)} %bitcast.122), calls=%async_computation.5 | async-start | bytes 1572864 | tf_op jit(solution)/shard_map/all_to_all | solution.py:150
  227.3 702.1 %all-gather.4.cloned.1.call-start = ((), (), s32[]{:S(2)}) async-start(), calls=%async_computation.8 | async-start | bytes 3170304 | tf_op jit(solution)/shard_map/all_gather | solution.py:12
  229.6 16.1 %copy-start.24 = (bf16[8,128,384]{2,1,0:T(8,128)(2,1)S(1)}, bf16[8,128,384]{2,1,0:T(8,128)(2,1)}, u32[]{:S(2)}) copy-start(bf16[8,128,384]{2,1,0:T(8,128)(2,1)} %copy.81) | copy-start | bytes 2359300
  243.4 4.4 copy-start.20
  247.7 3.3 copy-start.18
  248.2 3.6 copy-start.17
  249.5 39.8 %collective-permute-start.3 = (f32[1024,384]{0,1:T(8,128)}, f32[1024,384]{0,1:T(8,128)}, u32[]{:S(2)}, u32[]{:S(2)}) collective-permute-start(f32[1024,384]{0,1:T(8,128)} %pad_maximum_fusion.1), channel_id=1, source_target_pairs={{16,0},{32,16},{48,32},{64,48},{80,64},{96,80},{112,96},{128,112},... | collective-permute-start | bytes 4718600 | tf_op jit(solution)/shard_map/ppermute | solution.py:20
  253.7 4.9 copy-start.14
  291.8 643.4 %all-to-all-start.6 = ((bf16[8,128,384]{1,2,0:T(8,128)(2,1)}), bf16[8,128,384]{1,2,0:T(8,128)(2,1)S(1)}, u32[]{:S(2)}, u32[]{:S(2)}) async-start(bf16[8,128,384]{1,2,0:T(8,128)(2,1)} %copy_bitcast_fusion), calls=%async_computation.6 | async-start | bytes 1572864 | tf_op jit(solution)/shard_map/all_to_all | solution.py:153
  296.7 647.0 %reduce-scatter.4.cloned.1.call-start = ((), (), s32[]{:S(2)}) async-start(), calls=%async_computation.9 | async-start | bytes 2359296
  300.0 633.8 %copy-start.16 = (bf16[1,128,3072]{2,1,0:T(8,128)(2,1)S(1)}, bf16[1,128,3072]{2,1,0:T(8,128)(2,1)}, u32[]{:S(2)}) copy-start(bf16[1,128,3072]{2,1,0:T(8,128)(2,1)} %param.8) | copy-start | bytes 2359300
Sparse Core Ops, SparseCore 0:
  243.5 685.8 all-gather.3
  934.0 9.6 reduce-scatter.3
